TPU v7x, 512 devices: a whole 4x8x8 slice. The times are simulated.
512 devices in a mesh: blk: 32 (over y_hi, x, core), tp: 16 (over z, y_lo).
Axes of the slice: x: 4, y: 8 (y_hi: 4, y_lo: 2; y = y_hi * 2 + y_lo), z: 8, core: 2. Of those that a mesh axis runs over, the one named last changes fastest.
Arguments:
- tokens: bfloat16 [131072, 896], P(('blk', 'tp')), may hold values from -6 to 6
- cotangent: bfloat16 [131072, 896], P(('blk', 'tp')), may hold values from -0.59765625 to 0.59765625
- weights: bfloat16 [32, 2432, 3, 896], P('blk', 'tp'), may hold values from -6 to 6
- first_moment: bfloat16 [32, 2432, 3, 896], P('blk', 'tp'), may hold values from -0.1796875 to 0.1796875
- second_moment: bfloat16 [32, 2432, 3, 896], P('blk', 'tp'), may hold values from 0.0009994507 to 0.0099487305
Outputs:
- averaged: float32 [32, 2432, 3, 896], P('blk', 'tp')
All inputs are finite; a program needn't handle non-finite values.
Results may differ from a plain program's by a relative error of at most 0.0003.
Values may be sent and summed in bfloat16 or wider, within the bound.
A program may use at most 64 MiB of HBM per device.

v0:
```python
import jax
import jax.numpy as jnp
from jax import lax
from jax.sharding import PartitionSpec as P

STEP = 10


def shifted(block, axis, distance):
    devices = range(lax.axis_size(axis))
    route = [((i - distance) % len(devices), i) for i in devices]
    return lax.ppermute(block, axis, route)


def row_terms(xs, grads_out, rows, hidden_scale):
    width_scale = xs.shape[1] ** (-0.5)
    gate = (
        jnp.einsum("td,nd->tn", xs, rows[:, 0, :], preferred_element_type=jnp.float32) * width_scale
    )
    upper = (
        jnp.einsum("td,nd->tn", xs, rows[:, 1, :], preferred_element_type=jnp.float32) * width_scale
    )
    sigma = jax.nn.sigmoid(gate)
    swish = gate * sigma
    hidden = (swish * upper).astype(jnp.bfloat16)
    back = (
        jnp.einsum("td,nd->tn", grads_out, rows[:, 2, :], preferred_element_type=jnp.float32)
        * hidden_scale
    )
    dgate = (back * upper * sigma * (1.0 + gate * (1.0 - sigma))).astype(jnp.bfloat16)
    dupper = (back * swish).astype(jnp.bfloat16)
    grad_gate = jnp.einsum("tn,td->nd", dgate, xs, preferred_element_type=jnp.float32) * width_scale
    grad_upper = (
        jnp.einsum("tn,td->nd", dupper, xs, preferred_element_type=jnp.float32) * width_scale
    )
    grad_down = (
        jnp.einsum("tn,td->nd", hidden, grads_out, preferred_element_type=jnp.float32)
        * hidden_scale
    )
    return jnp.stack([grad_gate, grad_upper, grad_down], axis=1)


def on_device(tokens, cotangent, weights, first_moment, second_moment):
    own_rows = weights[0]
    local_units = own_rows.shape[0]
    hidden_scale = (local_units * lax.axis_size("tp")) ** (-0.5)
    all_tokens, all_cots = (
        lax.all_gather(tokens, "tp", axis=0, tiled=True),
        lax.all_gather(cotangent, "tp", axis=0, tiled=True),
    )
    grads = row_terms(all_tokens, all_cots, own_rows, hidden_scale)
    moment_one = 0.9 * first_moment[0].astype(jnp.float32) + 0.1 * grads
    moment_two = 0.95 * second_moment[0].astype(jnp.float32) + 0.05 * grads * grads
    correct_one = 1.0 - 0.9**STEP
    correct_two = 1.0 - 0.95**STEP
    master = own_rows.astype(jnp.float32)
    step_size = moment_one / correct_one / (jnp.sqrt(moment_two / correct_two) + 1e-08)
    updated = (master - 0.1 * (step_size + 0.1 * master))[None]
    previous = shifted(updated, "blk", 1)
    following = shifted(updated, "blk", -1)
    return (previous + updated + following) / 3.0


def solution(mesh):
    in_specs = (
        P(("blk", "tp"), None),
        P(("blk", "tp"), None),
        P("blk", "tp", None, None),
        P("blk", "tp", None, None),
        P("blk", "tp", None, None),
    )
    out_specs = P("blk", "tp", None, None)
    return jax.shard_map(
        on_device, mesh=mesh, in_specs=in_specs, out_specs=out_specs, check_vma=False
    )
```

profile of v0, /device:TPU:48, one launch (start us, length us, event | category | flops | bytes accessed | tf_op | source)
XLA Modules:
  0.0 416.1 jit_solution(5356604273082415112)
XLA Ops:
  6.5 0.0 all-gather.5.cloned.1.call-start
  6.5 0.7 all-gather.5.cloned.1.call-update
  7.3 0.0 all-gather.3.cloned.1.call-start
  7.3 0.7 all-gather.3.cloned.1.call-update
  8.0 171.3 %all-gather.5.cloned.1.call-done = bf16[4096,896]{1,0:T(8,128)(2,1)} async-done(((bf16[256,896]{1,0:T(8,128)(2,1)}), bf16[4096,896]{1,0:T(8,128)(2,1)}) %all-gather.5.cloned.1.call-update) | async-done | bytes 7340048 | tf_op jit(solution)/shard_map/all_gather | solution.py:48
  179.3 0.0 copy-start
  179.3 0.0 copy-start.3
  179.3 6.1 %convolution_multiply_fusion.1 = f32[4096,152]{0,1:T(8,128)S(1)} fusion(bf16[4096,896]{1,0:T(8,128)(2,1)} %all-gather.5.cloned.1.call-done, bf16[152,3,896]{2,0,1:T(8,128)(2,1)} %bitcast.24), kind=kOutput, calls=%fused_computation.1 | convolution fusion | flops 1116307456 | bytes 10102784 | tf_op jit(solution)/shard_map/td,nd->tn/dot_general | solution.py:21
  185.4 0.0 copy-done
  185.4 0.0 copy-done.3
  185.4 4.3 %convolution_multiply_fusion = f32[4096,152]{0,1:T(8,128)} fusion(bf16[4096,896]{1,0:T(8,128)(2,1)S(1)} %copy-done, bf16[152,3,896]{2,0,1:T(8,128)(2,1)S(1)} %bitcast.25), kind=kOutput, calls=%fused_computation | convolution fusion | flops 1116307456 | bytes 10102784 | tf_op jit(solution)/shard_map/td,nd->tn/dot_general | solution.py:18
  189.8 156.4 %all-gather.3.cloned.1.call-done = bf16[4096,896]{1,0:T(8,128)(2,1)} async-done(((bf16[256,896]{1,0:T(8,128)(2,1)}), bf16[4096,896]{1,0:T(8,128)(2,1)}) %all-gather.3.cloned.1.call-update) | async-done | bytes 7340048 | tf_op jit(solution)/shard_map/all_gather | solution.py:49
  346.2 0.0 copy-start.1
  346.2 0.0 copy-start.2
  346.2 0.0 slice-start
  346.2 6.1 %convolution_multiply_fusion.2 = f32[4096,152]{0,1:T(8,128)S(1)} fusion(bf16[4096,896]{1,0:T(8,128)(2,1)} %all-gather.3.cloned.1.call-done, bf16[152,3,896]{2,0,1:T(8,128)(2,1)S(1)} %bitcast.26), kind=kOutput, calls=%fused_computation.2 | convolution fusion | flops 1116307456 | bytes 10102784 | tf_op jit(solution)/shard_map/td,nd->tn/dot_general | solution.py:27
  352.3 0.0 copy-done.1
  352.3 0.0 copy-done.2
  352.3 0.0 slice-start.1
  352.3 1.7 fusion.12
  354.0 0.0 slice-done
  354.0 0.4 slice-done.1
  354.4 1.7 fusion.14
  356.1 0.0 copy-start.4
  356.1 0.0 copy-start.5
  356.1 1.8 fusion.16
  358.0 0.0 copy-done.4
  358.0 0.0 copy-done.5
  358.0 1.4 convert_subtract_fusion
  359.4 5.3 %collective-permute-start.1 = (f32[1,152,3,896]{3,1,2,0:T(8,128)S(1)}, f32[1,152,3,896]{3,1,2,0:T(8,128)S(1)}, u32[]{:S(2)}, u32[]{:S(2)}) collective-permute-start(f32[1,152,3,896]{3,1,2,0:T(8,128)S(1)} %convert_subtract_fusion), channel_id=1, source_target_pairs={{16,0},{32,16},{48,32},{64,48},{80,64},{96,80},{112,96},{128,112},... | collective-permute-start | bytes 4902920 | tf_op jit(solution)/shard_map/ppermute | solution.py:12
  364.7 1.9 collective-permute-start
  366.6 33.9 %collective-permute-done.1 = f32[1,152,3,896]{3,1,2,0:T(8,128)S(1)} collective-permute-done((f32[1,152,3,896]{3,1,2,0:T(8,128)S(1)}, f32[1,152,3,896]{3,1,2,0:T(8,128)S(1)}, u32[]{:S(2)}, u32[]{:S(2)}) %collective-permute-start.1) | collective-permute-done | bytes 1634336 | tf_op jit(solution)/shard_map/ppermute | solution.py:12
  400.5 7.2 %collective-permute-done = f32[1,152,3,896]{3,1,2,0:T(8,128)S(1)} collective-permute-done((f32[1,152,3,896]{3,1,2,0:T(8,128)S(1)}, f32[1,152,3,896]{3,1,2,0:T(8,128)S(1)}, u32[]{:S(2)}, u32[]{:S(2)}) %collective-permute-start) | collective-permute-done | bytes 1634336 | tf_op jit(solution)/shard_map/ppermute | solution.py:12
  407.7 1.5 add_multiply_fusion
  (1 shorter events, 0.0 us)
Async XLA Ops:
  6.5 172.8 %all-gather.5.cloned.1.call-start = ((), (), s32[]{:S(2)}) async-start(), calls=%async_computation.1 | async-start | bytes 7798784 | tf_op jit(solution)/shard_map/all_gather | solution.py:48
  7.3 338.9 %all-gather.3.cloned.1.call-start = ((), (), s32[]{:S(2)}) async-start(), calls=%async_computation | async-start | bytes 7798784 | tf_op jit(solution)/shard_map/all_gather | solution.py:49
  179.3 6.1 %copy-start = (bf16[4096,896]{1,0:T(8,128)(2,1)S(1)}, bf16[4096,896]{1,0:T(8,128)(2,1)}, u32[]{:S(2)}) copy-start(bf16[4096,896]{1,0:T(8,128)(2,1)} %all-gather.5.cloned.1.call-done) | copy-start | bytes 22020100
  179.3 6.1 %copy-start.3 = (bf16[1,152,3,896]{3,1,2,0:T(8,128)(2,1)S(1)}, bf16[1,152,3,896]{3,1,2,0:T(8,128)(2,1)}, u32[]{:S(2)}) copy-start(bf16[1,152,3,896]{3,1,2,0:T(8,128)(2,1)} %param.7) | copy-start | bytes 2451460
  346.2 6.1 %copy-start.1 = (bf16[4096,896]{1,0:T(8,128)(2,1)S(1)}, bf16[4096,896]{1,0:T(8,128)(2,1)}, u32[]{:S(2)}) copy-start(bf16[4096,896]{1,0:T(8,128)(2,1)} %all-gather.3.cloned.1.call-done) | copy-start | bytes 22020100
  346.2 6.1 %copy-start.2 = (f32[4096,152]{0,1:T(8,128)S(1)}, f32[4096,152]{0,1:T(8,128)}, u32[]{:S(2)}) copy-start(f32[4096,152]{0,1:T(8,128)} %convolution_multiply_fusion) | copy-start | bytes 7471108
  346.2 7.8 %slice-start = ((s8[7340032]{0:T(1024)(128)(4,1)}), s8[4194304]{0:T(1024)(128)(4,1)S(1)}, s32[]{:S(2)}) async-start(s8[7340032]{0:T(1024)(128)(4,1)} %bitcast.22), calls=%async_computation.2 | async-start | bytes 8388608
  352.3 2.1 slice-start.1
  356.1 1.9 copy-start.4
  356.1 1.9 copy-start.5
  359.4 41.1 %collective-permute-start.1 = (f32[1,152,3,896]{3,1,2,0:T(8,128)S(1)}, f32[1,152,3,896]{3,1,2,0:T(8,128)S(1)}, u32[]{:S(2)}, u32[]{:S(2)}) collective-permute-start(f32[1,152,3,896]{3,1,2,0:T(8,128)S(1)} %convert_subtract_fusion), channel_id=1, source_target_pairs={{16,0},{32,16},{48,32},{64,48},{80,64},{96,80},{112,96},{128,112},... | collective-permute-start | bytes 4902920 | tf_op jit(solution)/shard_map/ppermute | solution.py:12
  364.7 43.0 %collective-permute-start = (f32[1,152,3,896]{3,1,2,0:T(8,128)S(1)}, f32[1,152,3,896]{3,1,2,0:T(8,128)S(1)}, u32[]{:S(2)}, u32[]{:S(2)}) collective-permute-start(f32[1,152,3,896]{3,1,2,0:T(8,128)S(1)} %convert_subtract_fusion), channel_id=1, source_target_pairs={{496,0},{0,16},{16,32},{32,48},{48,64},{64,80},{80,96},{96,112},{1... | collective-permute-start | bytes 4902920 | tf_op jit(solution)/shard_map/ppermute | solution.py:12
Sparse Core Ops, SparseCore 0:
  9.4 169.8 all-gather.4
  181.4 164.7 all-gather.2
where the time goes:
time: 416 us
  waiting for transfers between devices  370 us (89%)
  matrix products  21.7 us (5%)
  between operations  13.5 us (3%)
  starting transfers between devices  7.25 us (2%)
    all_gather x1, waiting for transfers between devices, on_device(): lax.all_gather(tokens, 'tp', axis=0, tiled=True)  171 us
    all_gather x1, waiting for transfers between devices, on_device(): lax.all_gather(cotangent, 'tp', axis=0, tiled=True)  156 us
    ppermute x2, waiting for transfers between devices, shifted(): return lax.ppermute(block, axis, route)  41.1 us
  transfers between devices with their start and end apart: 4, of which 4 were waited for; matrix products, arithmetic and copies ran while one was open for 3% of the time, Pallas kernels for 0%

commit v1 on v0

--- a/solution.py
+++ b/solution.py
@@ -4,6 +4,13 @@
 from jax.sharding import PartitionSpec as P
 
 STEP = 10
+
+
+def gather_over(x, name, d):
+    count = lax.axis_size(name)
+    tiles = jnp.stack([x for _ in range(count)])
+    tiles = lax.all_to_all(tiles, name, split_axis=0, concat_axis=0)
+    return jnp.concatenate(tiles, axis=d)
 
 
 def shifted(block, axis, distance):
@@ -45,7 +52,7 @@
     local_units = own_rows.shape[0]
     hidden_scale = (local_units * lax.axis_size("tp")) ** (-0.5)
     all_tokens, all_cots = (
-        lax.all_gather(tokens, "tp", axis=0, tiled=True),
+        gather_over(tokens, "tp", 0),
         lax.all_gather(cotangent, "tp", axis=0, tiled=True),
     )
     grads = row_terms(all_tokens, all_cots, own_rows, hidden_scale)

time: 416 us -> 368 us (0.88)
  the two profiles are of different devices: /device:TPU:48 before, /device:TPU:72 now
where the time goes in v1:
time: 368 us
  waiting for transfers between devices  295 us (80%)
  matrix products  31 us (8%)
  starting transfers between devices  20.9 us (6%)
  between operations  13.5 us (4%)
  local copies, waits for them, and re-layouts  5 us (1%)
    all_to_all x1, waiting for transfers between devices, gather_over(): tiles = lax.all_to_all(tiles, name, split_axis=0, concat_axis=0)  205 us
    all_gather x1, waiting for transfers between devices, on_device(): lax.all_gather(cotangent, 'tp', axis=0, tiled=True)  47.5 us
    ppermute x2, waiting for transfers between devices, shifted(): return lax.ppermute(block, axis, route)  40.9 us
    all_to_all x1, starting transfers between devices, gather_over(): tiles = lax.all_to_all(tiles, name, split_axis=0, concat_axis=0)  11 us
    ppermute x2, starting transfers between devices, shifted(): return lax.ppermute(block, axis, route)  9.82 us
    dot_general x1, matrix products, row_terms(): jnp.einsum('td,nd->tn', xs, rows[:, 0, :], preferred_element_type=jnp.flo...  7.38 us
  transfers between devices with their start and end apart: 4, of which 4 were waited for; matrix products, arithmetic and copies ran while one was open for 4% of the time, Pallas kernels for 0%

profile of v1, /device:TPU:72, one launch (start us, length us, event | category | flops | bytes accessed | tf_op | source)
XLA Modules:
  0.0 367.9 jit_solution(7087371173608720490)
XLA Ops:
  6.5 5.0 %stack.10 = bf16[16,256,896]{2,1,0:T(8,128)(2,1)} broadcast(bf16[256,896]{1,0:T(8,128)(2,1)} %param.5), dimensions={1,2} | broadcast | bytes 7798784 | tf_op jit(solution)/shard_map/stack | solution.py:11
  11.5 0.0 copy-start.1
  11.5 11.0 %all-to-all-start = ((bf16[16,256,896]{2,1,0:T(8,128)(2,1)}), bf16[16,256,896]{2,1,0:T(8,128)(2,1)}, u32[]{:S(2)}, u32[]{:S(2)}) async-start(bf16[16,256,896]{2,1,0:T(8,128)(2,1)} %stack.10), calls=%async_computation | async-start | bytes 14680064 | tf_op jit(solution)/shard_map/all_to_all | solution.py:12
  22.5 0.0 all-gather.2.cloned.1.call-start
  22.6 0.7 all-gather.2.cloned.1.call-update
  23.3 205.5 %all-to-all-done = bf16[16,256,896]{2,1,0:T(8,128)(2,1)} async-done(((bf16[16,256,896]{2,1,0:T(8,128)(2,1)}), bf16[16,256,896]{2,1,0:T(8,128)(2,1)}, u32[]{:S(2)}, u32[]{:S(2)}) %all-to-all-start) | async-done | bytes 7340064 | tf_op jit(solution)/shard_map/all_to_all | solution.py:12
  228.7 0.0 copy-done.1
  228.7 6.0 %convolution_multiply_fusion.1 = f32[4096,152]{0,1:T(8,128)S(1)} fusion(bf16[4096,896]{1,0:T(8,128)(2,1)} %bitcast.2, bf16[152,3,896]{2,0,1:T(8,128)(2,1)S(1)} %bitcast.25), kind=kOutput, calls=%fused_computation.1 | convolution fusion | flops 1116307456 | bytes 10102784 | tf_op jit(solution)/shard_map/td,nd->tn/dot_general | solution.py:28
  234.7 7.4 %convolution_multiply_fusion = f32[4096,152]{0,1:T(8,128)} fusion(bf16[4096,896]{1,0:T(8,128)(2,1)} %bitcast.2, bf16[152,3,896]{2,0,1:T(8,128)(2,1)S(1)} %bitcast.26), kind=kOutput, calls=%fused_computation | convolution fusion | flops 1116307456 | bytes 10102784 | tf_op jit(solution)/shard_map/td,nd->tn/dot_general | solution.py:25
  242.1 47.5 %all-gather.2.cloned.1.call-done = bf16[4096,896]{1,0:T(8,128)(2,1)} async-done(((bf16[256,896]{1,0:T(8,128)(2,1)}), bf16[4096,896]{1,0:T(8,128)(2,1)}) %all-gather.2.cloned.1.call-update) | async-done | bytes 7340048 | tf_op jit(solution)/shard_map/all_gather | solution.py:56
  289.5 0.0 copy-start
  289.5 6.1 %convolution_multiply_fusion.2 = f32[4096,152]{0,1:T(8,128)S(1)} fusion(bf16[4096,896]{1,0:T(8,128)(2,1)} %all-gather.2.cloned.1.call-done, bf16[152,3,896]{2,0,1:T(8,128)(2,1)S(1)} %bitcast.27), kind=kOutput, calls=%fused_computation.2 | convolution fusion | flops 1116307456 | bytes 10102784 | tf_op jit(solution)/shard_map/td,nd->tn/dot_general | solution.py:34
  295.6 0.0 copy-done
  295.6 0.0 slice-start
  295.6 4.9 %fusion.14 = f32[1,152,1,896]{3,1,2,0:T(8,128)S(1)} fusion(bf16[4096,896]{1,0:T(8,128)(2,1)} %bitcast.2, f32[4096,152]{0,1:T(8,128)S(1)} %convolution_multiply_fusion.2, f32[4096,152]{0,1:T(8,128)S(1)} %copy-done), kind=kOutput, calls=%fused_computation.26 | convolution fusion | flops 1119556608 | bytes 12865536 | tf_op jit(solution)/shard_map/tn,td->nd/dot_general | solution.py:41
  300.5 0.0 slice-start.1
  300.5 5.1 %fusion.16 = f32[1,152,1,896]{3,1,2,0:T(8,128)S(1)} fusion(bf16[4096,896]{1,0:T(8,128)(2,1)} %bitcast.2, f32[4096,152]{0,1:T(8,128)S(1)} %copy-done, f32[4096,152]{0,1:T(8,128)S(1)} %convolution_multiply_fusion.2, f32[4096,152]{0,1:T(8,128)S(1)} %convolution_multiply_fusion.1), kind=kOutput, calls=%fused_computation.28 | convolution fusion | flops 1122046976 | bytes 15355904 | tf_op jit(solution)/shard_map/tn,td->nd/dot_general | solution.py:39
  305.6 0.0 slice-done
  305.6 0.0 slice-done.1
  305.6 0.0 copy-start.2
  305.6 0.0 copy-start.3
  305.7 1.7 fusion.12
  307.3 0.0 copy-done.2
  307.3 0.0 copy-done.3
  307.4 1.4 convert_subtract_fusion
  308.8 7.9 %collective-permute-start.1 = (f32[1,152,3,896]{3,1,2,0:T(8,128)S(1)}, f32[1,152,3,896]{3,1,2,0:T(8,128)S(1)}, u32[]{:S(2)}, u32[]{:S(2)}) collective-permute-start(f32[1,152,3,896]{3,1,2,0:T(8,128)S(1)} %convert_subtract_fusion), channel_id=1, source_target_pairs={{16,0},{32,16},{48,32},{64,48},{80,64},{96,80},{112,96},{128,112},... | collective-permute-start | bytes 4902920 | tf_op jit(solution)/shard_map/ppermute | solution.py:19
  316.7 1.9 collective-permute-start
  318.6 32.9 %collective-permute-done.1 = f32[1,152,3,896]{3,1,2,0:T(8,128)S(1)} collective-permute-done((f32[1,152,3,896]{3,1,2,0:T(8,128)S(1)}, f32[1,152,3,896]{3,1,2,0:T(8,128)S(1)}, u32[]{:S(2)}, u32[]{:S(2)}) %collective-permute-start.1) | collective-permute-done | bytes 1634336 | tf_op jit(solution)/shard_map/ppermute | solution.py:19
  351.5 8.0 %collective-permute-done = f32[1,152,3,896]{3,1,2,0:T(8,128)S(1)} collective-permute-done((f32[1,152,3,896]{3,1,2,0:T(8,128)S(1)}, f32[1,152,3,896]{3,1,2,0:T(8,128)S(1)}, u32[]{:S(2)}, u32[]{:S(2)}) %collective-permute-start) | collective-permute-done | bytes 1634336 | tf_op jit(solution)/shard_map/ppermute | solution.py:19
  359.5 1.5 add_multiply_fusion
  (1 shorter events, 0.0 us)
Async XLA Ops:
  11.5 217.2 %copy-start.1 = (bf16[1,152,3,896]{3,1,2,0:T(8,128)(2,1)S(1)}, bf16[1,152,3,896]{3,1,2,0:T(8,128)(2,1)}, u32[]{:S(2)}) copy-start(bf16[1,152,3,896]{3,1,2,0:T(8,128)(2,1)} %param.7) | copy-start | bytes 2451460
  11.5 217.2 %all-to-all-start = ((bf16[16,256,896]{2,1,0:T(8,128)(2,1)}), bf16[16,256,896]{2,1,0:T(8,128)(2,1)}, u32[]{:S(2)}, u32[]{:S(2)}) async-start(bf16[16,256,896]{2,1,0:T(8,128)(2,1)} %stack.10), calls=%async_computation | async-start | bytes 14680064 | tf_op jit(solution)/shard_map/all_to_all | solution.py:12
  22.5 267.0 %all-gather.2.cloned.1.call-start = ((), (), s32[]{:S(2)}) async-start(), calls=%async_computation.1 | async-start | bytes 7798784 | tf_op jit(solution)/shard_map/all_gather | solution.py:56
  289.5 6.1 %copy-start = (f32[4096,152]{0,1:T(8,128)S(1)}, f32[4096,152]{0,1:T(8,128)}, u32[]{:S(2)}) copy-start(f32[4096,152]{0,1:T(8,128)} %convolution_multiply_fusion) | copy-start | bytes 7471108
  295.6 10.0 %slice-start = ((s8[7340032]{0:T(1024)(128)(4,1)}), s8[4194304]{0:T(1024)(128)(4,1)S(1)}, s32[]{:S(2)}) async-start(s8[7340032]{0:T(1024)(128)(4,1)} %bitcast.23), calls=%async_computation.2 | async-start | bytes 8388608
  300.5 5.1 %slice-start.1 = ((s8[7340032]{0:T(1024)(128)(4,1)}), s8[3145728]{0:T(1024)(128)(4,1)S(1)}, s32[]{:S(2)}) async-start(s8[7340032]{0:T(1024)(128)(4,1)} %bitcast.23), calls=%async_computation.3 | async-start | bytes 6291456
  305.6 1.7 copy-start.2
  305.6 1.7 copy-start.3
  308.8 42.7 %collective-permute-start.1 = (f32[1,152,3,896]{3,1,2,0:T(8,128)S(1)}, f32[1,152,3,896]{3,1,2,0:T(8,128)S(1)}, u32[]{:S(2)}, u32[]{:S(2)}) collective-permute-start(f32[1,152,3,896]{3,1,2,0:T(8,128)S(1)} %convert_subtract_fusion), channel_id=1, source_target_pairs={{16,0},{32,16},{48,32},{64,48},{80,64},{96,80},{112,96},{128,112},... | collective-permute-start | bytes 4902920 | tf_op jit(solution)/shard_map/ppermute | solution.py:19
  316.7 42.9 %collective-permute-start = (f32[1,152,3,896]{3,1,2,0:T(8,128)S(1)}, f32[1,152,3,896]{3,1,2,0:T(8,128)S(1)}, u32[]{:S(2)}, u32[]{:S(2)}) collective-permute-start(f32[1,152,3,896]{3,1,2,0:T(8,128)S(1)} %convert_subtract_fusion), channel_id=1, source_target_pairs={{496,0},{0,16},{16,32},{32,48},{48,64},{64,80},{80,96},{96,112},{1... | collective-permute-start | bytes 4902920 | tf_op jit(solution)/shard_map/ppermute | solution.py:19
Sparse Core Ops, SparseCore 0:
  25.4 264.0 all-gather.1
